TPU v7x, 512 devices: a whole 4x4x16 slice. The times are simulated.
512 devices in a mesh: seq: 32 (over z, core), mp: 16 (over y, x).
Axes of the slice: x: 4, y: 4, z: 16, core: 2. Of those that a mesh axis runs over, the one named last changes fastest.
Arguments:
- continued_prompt_entries: bfloat16 [4096, 4096], P('seq', 'mp'), may hold values from -6 to 6
- padded_prompt_entries: bfloat16 [4096, 4096], P('seq', 'mp'), may hold values from -6 to 6
- prompt_live_extents: int32 [64], P('seq'), may hold values from 8 to 64, as said below
- preceding_entry_line: bfloat16 [4096], P('mp'), may hold values from -6 to 6
- carried_memory: float32 [64, 64, 64], P('mp'), may hold values from -24 to 24
- token_mixing_ratios: float32 [5, 4096], replicated, may hold values from 0.05 to 0.95
- acceptance_transform: bfloat16 [4096, 4096], P('seq', 'mp'), may hold values from -0.09375 to 0.09375
- lookup_transform: bfloat16 [4096, 4096], P('seq', 'mp'), may hold values from -0.09375 to 0.09375
- payload_transform: bfloat16 [4096, 4096], P('seq', 'mp'), may hold values from -0.09375 to 0.09375
- gating_transform: bfloat16 [4096, 4096], P('seq', 'mp'), may hold values from -0.09375 to 0.09375
- fading_baseline: float32 [4096], P('mp'), may hold values from -10 to -3.5
- fading_left_factor: bfloat16 [4096, 128], replicated, may hold values from -0.09375 to 0.09375
- fading_right_factor: bfloat16 [128, 4096], P(None, 'mp'), may hold values from -0.5 to 0.5
- present_reward: float32 [64, 64], P('mp'), may hold values from -3 to 3
- group_layer_scaling: float32 [4096], P('mp'), may hold values from 0.5 to 1.5
- group_layer_shift_term: float32 [4096], P('mp'), may hold values from -1.8 to 1.8
- final_transform: bfloat16 [4096, 4096], P('mp', 'seq'), may hold values from -0.09375 to 0.09375
Outputs:
- mixed: bfloat16 [32, 256, 4096], P('seq', 'mp')
- span_states: float32 [32, 64, 64, 64], P('seq', 'mp')
- request_states: float32 [64, 64, 64, 64], P('seq', 'mp')
Inputs may be any that keep to these rules, and one draw needn't show every extreme that they name: `prompt_live_extents`: some request has all 64 rows live.
All inputs are finite; a program needn't handle non-finite values.
Results may differ from a plain program's by a relative error of at most 0.0076.
Values may be sent and summed in bfloat16 or wider, within the bound.
A program may use at most 64 MiB of HBM per device.

v0:
```python
import jax
import jax.numpy as jnp
from jax import lax
from jax.sharding import PartitionSpec as P

BLK = 64
SEQ = ("z", "core")
norm_eps = 0.00064
highest = lax.Precision.HIGHEST


def seq_index():
    return lax.axis_index("z") * lax.axis_size("core") + lax.axis_index("core")


def seq_shift(x, by, length):
    pairs = [(i, i + by) for i in range(length) if i + by < length]
    return lax.ppermute(x, SEQ, pairs)


def exclusive_prefix(value, start, length):
    mine = seq_index()
    arrived = seq_shift(value, 1, length)
    total = jax.tree.map(lambda got, first: jnp.where(mine == 0, first, got), arrived, start)
    step = 1
    while step < length:
        got = seq_shift(total, step, length)
        joined = combine(got, total)
        total = jax.tree.map(lambda new, old: jnp.where(mine >= step, new, old), joined, total)
        step *= 2
    return total


def mix_rows(current, previous, weight):
    here = current.astype(jnp.float32)
    return (here + weight[None, :] * (previous.astype(jnp.float32) - here)).astype(jnp.bfloat16)


def block_sweep(
    evolving_memory,
    acceptance_entries,
    lookup_entries,
    payload_entries,
    log_fading_amount,
    diagonal_reward,
):
    inclusive = jnp.cumsum(log_fading_amount, axis=0)
    exclusive = inclusive - log_fading_amount
    recept_scaled = acceptance_entries * jnp.exp(exclusive)
    keys_scaled = lookup_entries * jnp.exp(-inclusive)
    scores = jnp.einsum("ihc,jhc->hij", recept_scaled, keys_scaled, precision=highest)
    count = acceptance_entries.shape[0]
    row_index = lax.broadcasted_iota(jnp.int32, (count, count), 0)
    col_index = lax.broadcasted_iota(jnp.int32, (count, count), 1)
    scores = jnp.where((row_index > col_index)[None], scores, 0.0)
    diagonal_contribution = jnp.sum(
        acceptance_entries * diagonal_reward[None] * lookup_entries, axis=-1, keepdims=True
    )
    answer_lines = (
        jnp.einsum("hij,jhd->ihd", scores, payload_entries, precision=highest)
        + diagonal_contribution * payload_entries
    )
    answer_lines = answer_lines + jnp.einsum(
        "ihc,hcd->ihd", recept_scaled, evolving_memory, precision=highest
    )
    total = inclusive[-1]
    carried = lookup_entries * jnp.exp(total[None] - inclusive)
    new_state = jnp.exp(total)[:, :, None] * evolving_memory + jnp.einsum(
        "jhc,jhd->hcd", carried, payload_entries, precision=highest
    )
    return (new_state, answer_lines)


def continued_recurrence(
    acceptance_entries, lookup_entries, payload_entries, log_fading_amount, diagonal_reward
):
    length, per_group_view, embedding_dimension = acceptance_entries.shape
    blocks = length // BLK

    def step(evolving_memory, entry_lines):
        return block_sweep(
            evolving_memory,
            entry_lines[0],
            entry_lines[1],
            entry_lines[2],
            entry_lines[3],
            diagonal_reward,
        )

    shaped = tuple(
        (
            a.reshape(blocks, BLK, per_group_view, embedding_dimension)
            for a in (acceptance_entries, lookup_entries, payload_entries, log_fading_amount)
        )
    )
    evolving_memory, results = lax.scan(
        step,
        jnp.zeros((per_group_view, embedding_dimension, embedding_dimension), jnp.float32),
        shaped,
    )
    return (evolving_memory, results.reshape(length, per_group_view, embedding_dimension))


def combine(earlier, later):
    return (earlier[0] + later[0], jnp.exp(later[0])[:, :, None] * earlier[1] + later[1])


def shifted_rows(current, edge_row, long_rows, requests, slot_rows):
    feature_part = current.shape[1]
    long_prev = jnp.concatenate([edge_row, current[: long_rows - 1]], axis=0)
    short_view = current[long_rows:].reshape(requests, slot_rows, feature_part)
    short_prev = jnp.concatenate(
        [jnp.zeros((requests, 1, feature_part), current.dtype), short_view[:, :-1]], axis=1
    )
    short_prev = short_prev.reshape(requests * slot_rows, feature_part)
    return jnp.concatenate([long_prev, short_prev], axis=0)


def on_device(
    continued_prompt_entries,
    padded_prompt_entries,
    prompt_live_extents,
    preceding_entry_line,
    carried_memory,
    token_mixing_ratios,
    acceptance_transform,
    lookup_transform,
    payload_transform,
    gating_transform,
    fading_baseline,
    fading_left_factor,
    fading_right_factor,
    present_reward,
    group_layer_scaling,
    group_layer_shift_term,
    final_transform,
):
    long_rows = continued_prompt_entries.shape[0]
    requests = prompt_live_extents.shape[0]
    slot_rows = padded_prompt_entries.shape[0] // requests
    per_group_view, embedding_dimension = present_reward.shape
    seq_count = lax.axis_size("z") * lax.axis_size("core")
    arrived = seq_shift(continued_prompt_entries[-1:], 1, seq_count)
    first = seq_index() == 0
    edge_row = jnp.where(first, preceding_entry_line[None, :], arrived)
    stacked = jnp.concatenate([continued_prompt_entries, padded_prompt_entries, edge_row], axis=0)
    stacked = lax.all_gather(stacked, "mp", axis=1, tiled=True)
    current = stacked[: long_rows + padded_prompt_entries.shape[0]]
    edge_full = stacked[-1:]
    previous = shifted_rows(current, edge_full, long_rows, requests, slot_rows)
    mixes = [mix_rows(current, previous, token_mixing_ratios[index]) for index in range(5)]
    total_rows = current.shape[0]
    columns = acceptance_transform.shape[1]
    blocks = jnp.stack(
        [
            acceptance_transform,
            lookup_transform,
            payload_transform,
            gating_transform,
            final_transform.T,
        ],
        axis=0,
    )
    blocks = lax.all_gather(lax.all_gather(blocks, "z"), "core")
    cores, chips, kinds, depth, width = blocks.shape
    blocks = jnp.transpose(blocks, (2, 1, 0, 3, 4)).reshape(kinds, chips * cores * depth, width)
    pieces = tuple((blocks[index] for index in range(4)))
    acceptance_entries, lookup_entries, payload_entries, gate = tuple(
        (
            jnp.dot(source, piece, preferred_element_type=jnp.float32)
            for source, piece in zip(mixes[:4], pieces)
        )
    )
    squeezed = jnp.tanh(
        jnp.dot(mixes[4], fading_left_factor, preferred_element_type=jnp.float32)
    ).astype(jnp.bfloat16)
    log_fading_amount = -jnp.exp(
        fading_baseline[None, :]
        + jnp.dot(squeezed, fading_right_factor, preferred_element_type=jnp.float32)
    )
    recept3, keys3, values3, decay3 = [
        a.reshape(total_rows, per_group_view, embedding_dimension)
        for a in (acceptance_entries, lookup_entries, payload_entries, log_fading_amount)
    ]
    local_state, long_out = continued_recurrence(
        recept3[:long_rows],
        keys3[:long_rows],
        values3[:long_rows],
        decay3[:long_rows],
        present_reward,
    )
    long_decay = decay3[:long_rows]
    group_total = jnp.sum(long_decay, axis=0)
    start = (jnp.zeros((per_group_view, embedding_dimension), jnp.float32), carried_memory)
    _, incoming = exclusive_prefix((group_total, local_state), start, seq_count)
    before_row = jnp.cumsum(long_decay, axis=0) - long_decay
    long_out = long_out + jnp.einsum(
        "ihc,hcd->ihd", recept3[:long_rows] * jnp.exp(before_row), incoming, precision=highest
    )
    span_end = jnp.exp(group_total)[:, :, None] * incoming + local_state
    live_rows = (
        lax.broadcasted_iota(jnp.int32, (requests, slot_rows), 1) < prompt_live_extents[:, None]
    )
    live_flat = live_rows.reshape(requests * slot_rows).astype(jnp.float32)[:, None, None]
    short_shape = (requests, slot_rows, per_group_view, embedding_dimension)
    short_recept = recept3[long_rows:].reshape(short_shape)
    short_keys = (keys3[long_rows:] * live_flat).reshape(short_shape)
    short_values = values3[long_rows:].reshape(short_shape)
    short_decay = (decay3[long_rows:] * live_flat).reshape(short_shape)
    zeroed_memory = jnp.zeros(
        (per_group_view, embedding_dimension, embedding_dimension), jnp.float32
    )

    def request_pass(acceptance_lines, lookup_table, payload_table, fading_table):
        return block_sweep(
            zeroed_memory,
            acceptance_lines,
            lookup_table,
            payload_table,
            fading_table,
            present_reward,
        )

    request_states, short_out = jax.vmap(request_pass)(
        short_recept, short_keys, short_values, short_decay
    )
    wkv = jnp.concatenate(
        [long_out, short_out.reshape(requests * slot_rows, per_group_view, embedding_dimension)],
        axis=0,
    )
    mean = jnp.mean(wkv, axis=-1, keepdims=True)
    centred = wkv - mean
    variance = jnp.mean(centred * centred, axis=-1, keepdims=True)
    normed = (centred * lax.rsqrt(variance + norm_eps)).reshape(
        total_rows, columns
    ) * group_layer_scaling[None, :] + group_layer_shift_term[None, :]
    row_live = jnp.concatenate(
        [jnp.ones((long_rows,), dtype=bool), live_rows.reshape(requests * slot_rows)], axis=0
    )
    hidden = jnp.where(row_live[:, None], normed * jax.nn.silu(gate), 0.0).astype(jnp.bfloat16)
    full_out = blocks[4]
    mixed_rows = lax.psum_scatter(
        lax.dot_general(
            hidden, full_out, (((1,), (1,)), ((), ())), preferred_element_type=jnp.float32
        ),
        "mp",
        scatter_dimension=0,
        tiled=True,
    )
    return (mixed_rows.astype(jnp.bfloat16)[None], span_end[None], request_states)


def solution(mesh):
    placed = (
        P("seq", "mp"),
        P("seq", "mp"),
        P("seq"),
        P("mp"),
        P("mp", None, None),
        P(),
        P("seq", "mp"),
        P("seq", "mp"),
        P("seq", "mp"),
        P("seq", "mp"),
        P("mp"),
        P(),
        P(None, "mp"),
        P("mp", None),
        P("mp"),
        P("mp"),
        P("mp", "seq"),
    )
    devices = mesh.devices
    seq_devices, mp_devices = devices.shape
    mesh = jax.sharding.Mesh(devices.reshape(seq_devices // 2, 2, mp_devices), ("z", "core", "mp"))
    placed = tuple((P(*[SEQ if name == "seq" else name for name in spec]) for spec in placed))
    return jax.shard_map(
        on_device,
        mesh=mesh,
        in_specs=placed,
        out_specs=(P(SEQ, "mp", None), P(SEQ, "mp", None, None), P(SEQ, "mp", None, None)),
        check_vma=False,
    )
```

profile of v0, /device:TPU:2, one launch (start us, length us, event | category | flops | bytes accessed | tf_op | source)
XLA Modules:
  0.0 407.3 jit_solution(4726152788664702614)
XLA Ops:
  17.9 80.3 %all-gather.8.cloned.1.call-done = bf16[80,128,256]{2,1,0:T(8,128)(2,1)} async-done(((bf16[5,128,256]{2,1,0:T(8,128)(2,1)}), bf16[80,128,256]{2,1,0:T(8,128)(2,1)}) %all-gather.8.cloned.1.call-update) | async-done | bytes 5242896 | tf_op jit(solution)/shard_map/all_gather | solution.py:164
  99.8 60.9 %all-gather.6.cloned.1.call-done = bf16[257,4096]{1,0:T(8,128)(2,1)} async-done(((bf16[257,256]{1,0:T(8,128)(2,1)}), bf16[257,4096]{1,0:T(8,128)(2,1)}) %all-gather.6.cloned.1.call-update) | async-done | bytes 2105360 | tf_op jit(solution)/shard_map/all_gather | solution.py:147
  160.7 1.9 slice-done
  164.0 3.0 fusion.40
  169.3 4.1 %collective-permute-start.2 = (f32[4,64]{1,0:T(4,128)S(1)}, f32[4,64]{1,0:T(4,128)S(1)}, u32[]{:S(2)}, u32[]{:S(2)}) collective-permute-start(f32[4,64]{1,0:T(4,128)S(1)} %get-tuple-element.130), channel_id=1, source_target_pairs={{0,16},{16,32},{32,48},{48,64},{64,80},{80,96},{96,112},{112,128},... | collective-permute-start | bytes 3080 | tf_op jit(solution)/shard_map/ppermute | solution.py:18
  174.4 6.0 %collective-permute-start.3 = (f32[4,64]{1,0:T(4,128)S(1)}, f32[4,64]{1,0:T(4,128)S(1)}, u32[]{:S(2)}, u32[]{:S(2)}) collective-permute-start(f32[4,64]{1,0:T(4,128)S(1)} %get-tuple-element.128), channel_id=1, source_target_pairs={{0,32},{16,48},{32,64},{48,80},{64,96},{80,112},{96,128},{112,144}... | collective-permute-start | bytes 3080 | tf_op jit(solution)/shard_map/ppermute | solution.py:18
  181.8 5.2 %collective-permute-start.4 = (f32[4,64]{1,0:T(4,128)S(1)}, f32[4,64]{1,0:T(4,128)S(1)}, u32[]{:S(2)}, u32[]{:S(2)}) collective-permute-start(f32[4,64]{1,0:T(4,128)S(1)} %get-tuple-element.126), channel_id=1, source_target_pairs={{0,64},{16,80},{32,96},{48,112},{64,128},{80,144},{96,160},{112,17... | collective-permute-start | bytes 3080 | tf_op jit(solution)/shard_map/ppermute | solution.py:18
  188.2 13.1 %collective-permute-start.5 = (f32[4,64]{1,0:T(4,128)S(1)}, f32[4,64]{1,0:T(4,128)S(1)}, u32[]{:S(2)}, u32[]{:S(2)}) collective-permute-start(f32[4,64]{1,0:T(4,128)S(1)} %get-tuple-element.124), channel_id=1, source_target_pairs={{0,128},{16,144},{32,160},{48,176},{64,192},{80,208},{96,224},{112... | collective-permute-start | bytes 3080 | tf_op jit(solution)/shard_map/ppermute | solution.py:18
  201.4 6.2 %fusion.92 = (bf16[1,16,2,128,256]{4,3,0,1,2:T(8,128)(2,1)}, bf16[1,16,2,128,256]{4,3,0,1,2:T(8,128)(2,1)}, bf16[1,16,2,128,256]{4,3,0,1,2:T(8,128)(2,1)S(1)}, b...) fusion(bf16[5,16,2,128,256]{4,3,0,1,2:T(8,128)(2,1)} %bitcast.142), kind=kLoop, calls=%fused_computation.139 | loop fusion | bytes 20971520 | tf_op jit(solution)/shard_map/slice | solution.py:167
  217.1 13.2 %while.13 = (s32[]{:T(128)}, f32[4,64,64]{2,1,0:T(8,128)S(1)}, f32[2,64,4,64]{1,0,3,2:T(2,128)}, f32[2,64,4,64]{1,0,3,2:T(2,128)S(1)}, f32[2,64,4,64]{3,2,1,0:T(...) while((s32[]{:T(128)}, f32[4,64,64]{2,1,0:T(8,128)S(1)}, ...), condition=%wide.region_3.4_spmd.clone, body=%wide.region_0.3_spmd.clone.sunk | while | flops 51646208 | bytes 2444424 | solution.py:96
  219.4 4.3 %dynamic_update_slice.6 = f32[2,64,4,64]{1,0,3,2:T(2,128)} dynamic-update-slice(f32[2,64,4,64]{1,0,3,2:T(2,128)} %get-tuple-element.235, f32[1,64,4,64]{1,0,3,2:T(1,128)S(1)} %copy.218, s32[]{:T(128)S(6)} %copy.227, s32[]{:T(128)} %constant.28.clone.1..sunk, s32[]{:T(128)} %constant.28.clone.1..sunk, s32[]{:T(128)} %constant.28.clone.1..sunk) | dynamic-update-slice | bytes 131076 | tf_op jit(solution)/shard_map/while/body/jit(dynamic_update_index_in_dim)/dynamic_update_slice | solution.py:96
  226.1 4.3 %dynamic_update_slice.6 = f32[2,64,4,64]{1,0,3,2:T(2,128)} dynamic-update-slice(f32[2,64,4,64]{1,0,3,2:T(2,128)} %get-tuple-element.235, f32[1,64,4,64]{1,0,3,2:T(1,128)S(1)} %copy.218, s32[]{:T(128)S(6)} %copy.227, s32[]{:T(128)} %constant.28.clone.1..sunk, s32[]{:T(128)} %constant.28.clone.1..sunk, s32[]{:T(128)} %constant.28.clone.1..sunk) | dynamic-update-slice | bytes 131076 | tf_op jit(solution)/shard_map/while/body/jit(dynamic_update_index_in_dim)/dynamic_update_slice | solution.py:96
  236.5 2.1 exponential_multiply_fusion
  238.6 5.3 %collective-permute-start.8 = (f32[4,64,64]{2,1,0:T(8,128)S(1)}, f32[4,64,64]{2,1,0:T(8,128)S(1)}, u32[]{:S(2)}, u32[]{:S(2)}) collective-permute-start(f32[4,64,64]{2,1,0:T(8,128)S(1)} %add_select_fusion.4), channel_id=1, source_target_pairs={{0,32},{16,48},{32,64},{48,80},{64,96},{80,112},{96,128},{112,144}... | collective-permute-start | bytes 196616 | tf_op jit(solution)/shard_map/ppermute | solution.py:18
  244.9 2.5 collective-permute-done.8
  247.5 6.3 %collective-permute-start.9 = (f32[4,64,64]{2,1,0:T(8,128)S(1)}, f32[4,64,64]{2,1,0:T(8,128)S(1)}, u32[]{:S(2)}, u32[]{:S(2)}) collective-permute-start(f32[4,64,64]{2,1,0:T(8,128)S(1)} %add_select_fusion.3), channel_id=1, source_target_pairs={{0,64},{16,80},{32,96},{48,112},{64,128},{80,144},{96,160},{112,17... | collective-permute-start | bytes 196616 | tf_op jit(solution)/shard_map/ppermute | solution.py:18
  254.4 3.2 collective-permute-done.9
  257.7 12.6 %collective-permute-start.10 = (f32[4,64,64]{2,1,0:T(8,128)S(1)}, f32[4,64,64]{2,1,0:T(8,128)S(1)}, u32[]{:S(2)}, u32[]{:S(2)}) collective-permute-start(f32[4,64,64]{2,1,0:T(8,128)S(1)} %add_select_fusion.2), channel_id=1, source_target_pairs={{0,128},{16,144},{32,160},{48,176},{64,192},{80,208},{96,224},{112... | collective-permute-start | bytes 196616 | tf_op jit(solution)/shard_map/ppermute | solution.py:18
  273.0 13.9 %collective-permute-start.11 = (f32[4,64,64]{2,1,0:T(8,128)S(1)}, f32[4,64,64]{2,1,0:T(8,128)}, u32[]{:S(2)}, u32[]{:S(2)}) collective-permute-start(f32[4,64,64]{2,1,0:T(8,128)S(1)} %add_select_fusion.1), channel_id=1, source_target_pairs={{0,256},{16,272},{32,288},{48,304},{64,320},{80,336},{96,352},{112... | collective-permute-start | bytes 196616 | tf_op jit(solution)/shard_map/ppermute | solution.py:18
  289.5 3.3 copy.156
  296.4 1.8 concatenate.27
  302.4 1.8 copy.154
  307.5 7.5 %fusion.68 = f32[256,4096]{1,0:T(8,128)} fusion(bf16[4096,256]{1,0:T(8,128)(2,1)} %bitcast.145, f32[256,256]{1,0:T(8,128)} %copy.154, f32[256,256]{1,0:T(8,128)} %copy.153, f32[128,256]{1,0:T(8,128)} %concatenate.27, f32[128,256]{1,0:T(8,128)} %copy.151, bf16[4096,256]{1,0:T(8,128)(2,1)} %bitcast.146, f32[4096]{0:T(1024)S(1)} %bitcast.160, ...), kind=kOutput, calls=%fused_computation.84 | convolution fusion | flops 1086062592 | bytes 13396480 | tf_op jit(solution)/shard_map/dot_general | solution.py:243
  319.0 80.1 %reduce-scatter.2.cloned.1.call-done = f32[16,4096]{1,0:T(8,128)} async-done(((f32[256,4096]{1,0:T(8,128)}), f32[16,4096]{1,0:T(8,128)}) %reduce-scatter.2.cloned.1.call-update) | async-done | bytes 262160 | tf_op jit(solution)/shard_map/reduce_scatter | solution.py:242
  (199 shorter events, 62.9 us)
Async XLA Ops:
  7.2 156.8 %copy-start = (bf16[4096,128]{1,0:T(8,128)(2,1)S(1)}, bf16[4096,128]{1,0:T(8,128)(2,1)}, u32[]{:S(2)}) copy-start(bf16[4096,128]{1,0:T(8,128)(2,1)} %param.30) | copy-start | bytes 3145732
  7.2 91.1 %all-gather.8.cloned.1.call-start = ((), (), s32[]{:S(2)}) async-start(), calls=%async_computation.3 | async-start | bytes 5570560 | tf_op jit(solution)/shard_map/all_gather | solution.py:164
  12.4 148.3 %all-gather.6.cloned.1.call-start = ((), (), s32[]{:S(2)}) async-start(), calls=%async_computation.1 | async-start | bytes 2297856 | tf_op jit(solution)/shard_map/all_gather | solution.py:147
  13.1 2.5 collective-permute-start
  17.9 183.5 %all-gather.10.cloned.1.call-start = ((), (), s32[]{:S(2)}) async-start(), calls=%async_computation.4 | async-start | bytes 15728640 | tf_op jit(solution)/shard_map/all_gather | solution.py:164
  98.3 300.9 %reduce-scatter.2.cloned.1.call-start = ((), (), s32[]{:S(2)}) async-start(), calls=%async_computation.2 | async-start | bytes 4456448 | tf_op jit(solution)/shard_map/reduce_scatter | solution.py:242
  167.2 2.1 collective-permute-start.1
  169.3 5.1 %collective-permute-start.2 = (f32[4,64]{1,0:T(4,128)S(1)}, f32[4,64]{1,0:T(4,128)S(1)}, u32[]{:S(2)}, u32[]{:S(2)}) collective-permute-start(f32[4,64]{1,0:T(4,128)S(1)} %get-tuple-element.130), channel_id=1, source_target_pairs={{0,16},{16,32},{32,48},{48,64},{64,80},{80,96},{96,112},{112,128},... | collective-permute-start | bytes 3080 | tf_op jit(solution)/shard_map/ppermute | solution.py:18
  174.4 33.2 %copy-start.7 = (f32[2,64,4,64]{3,2,1,0:T(4,128)}, f32[2,64,4,64]{3,2,1,0:T(4,128)S(1)}, u32[]{:S(2)}) copy-start(f32[2,64,4,64]{3,2,1,0:T(4,128)S(1)} %copy.141) | copy-start | bytes 393220
  174.4 7.3 %collective-permute-start.3 = (f32[4,64]{1,0:T(4,128)S(1)}, f32[4,64]{1,0:T(4,128)S(1)}, u32[]{:S(2)}, u32[]{:S(2)}) collective-permute-start(f32[4,64]{1,0:T(4,128)S(1)} %get-tuple-element.128), channel_id=1, source_target_pairs={{0,32},{16,48},{32,64},{48,80},{64,96},{80,112},{96,128},{112,144}... | collective-permute-start | bytes 3080 | tf_op jit(solution)/shard_map/ppermute | solution.py:18
  181.8 6.5 %collective-permute-start.4 = (f32[4,64]{1,0:T(4,128)S(1)}, f32[4,64]{1,0:T(4,128)S(1)}, u32[]{:S(2)}, u32[]{:S(2)}) collective-permute-start(f32[4,64]{1,0:T(4,128)S(1)} %get-tuple-element.126), channel_id=1, source_target_pairs={{0,64},{16,80},{32,96},{48,112},{64,128},{80,144},{96,160},{112,17... | collective-permute-start | bytes 3080 | tf_op jit(solution)/shard_map/ppermute | solution.py:18
  188.2 43.4 %collective-permute-start.5 = (f32[4,64]{1,0:T(4,128)S(1)}, f32[4,64]{1,0:T(4,128)S(1)}, u32[]{:S(2)}, u32[]{:S(2)}) collective-permute-start(f32[4,64]{1,0:T(4,128)S(1)} %get-tuple-element.124), channel_id=1, source_target_pairs={{0,128},{16,144},{32,160},{48,176},{64,192},{80,208},{96,224},{112... | collective-permute-start | bytes 3080 | tf_op jit(solution)/shard_map/ppermute | solution.py:18
  230.3 3.7 collective-permute-start.6
  232.7 11.8 %copy-start.19 = (f32[128,256]{1,0:T(8,128)S(1)}, f32[128,256]{1,0:T(8,128)}, u32[]{:S(2)}) copy-start(f32[128,256]{1,0:T(8,128)} %get-tuple-element.152) | copy-start | bytes 393220
  235.0 3.5 collective-permute-start.7
  238.6 8.7 %collective-permute-start.8 = (f32[4,64,64]{2,1,0:T(8,128)S(1)}, f32[4,64,64]{2,1,0:T(8,128)S(1)}, u32[]{:S(2)}, u32[]{:S(2)}) collective-permute-start(f32[4,64,64]{2,1,0:T(8,128)S(1)} %add_select_fusion.4), channel_id=1, source_target_pairs={{0,32},{16,48},{32,64},{48,80},{64,96},{80,112},{96,128},{112,144}... | collective-permute-start | bytes 196616 | tf_op jit(solution)/shard_map/ppermute | solution.py:18
  244.8 43.8 %copy-start.5 = (f32[2,64,4,64]{1,3,2,0:T(8,128)}, f32[2,64,4,64]{1,3,2,0:T(8,128)S(1)}, u32[]{:S(2)}) copy-start(f32[2,64,4,64]{1,3,2,0:T(8,128)S(1)} %copy.145) | copy-start | bytes 393220
  247.5 10.1 %collective-permute-start.9 = (f32[4,64,64]{2,1,0:T(8,128)S(1)}, f32[4,64,64]{2,1,0:T(8,128)S(1)}, u32[]{:S(2)}, u32[]{:S(2)}) collective-permute-start(f32[4,64,64]{2,1,0:T(8,128)S(1)} %add_select_fusion.3), channel_id=1, source_target_pairs={{0,64},{16,80},{32,96},{48,112},{64,128},{80,144},{96,160},{112,17... | collective-permute-start | bytes 196616 | tf_op jit(solution)/shard_map/ppermute | solution.py:18
  257.7 15.1 %collective-permute-start.10 = (f32[4,64,64]{2,1,0:T(8,128)S(1)}, f32[4,64,64]{2,1,0:T(8,128)S(1)}, u32[]{:S(2)}, u32[]{:S(2)}) collective-permute-start(f32[4,64,64]{2,1,0:T(8,128)S(1)} %add_select_fusion.2), channel_id=1, source_target_pairs={{0,128},{16,144},{32,160},{48,176},{64,192},{80,208},{96,224},{112... | collective-permute-start | bytes 196616 | tf_op jit(solution)/shard_map/ppermute | solution.py:18
  273.0 19.8 %copy-start.9 = (f32[4,64,64]{2,1,0:T(8,128)}, f32[4,64,64]{2,1,0:T(8,128)S(1)}, u32[]{:S(2)}) copy-start(f32[4,64,64]{2,1,0:T(8,128)S(1)} %add_select_fusion.1) | copy-start | bytes 196612
  273.0 26.8 %collective-permute-start.11 = (f32[4,64,64]{2,1,0:T(8,128)S(1)}, f32[4,64,64]{2,1,0:T(8,128)}, u32[]{:S(2)}, u32[]{:S(2)}) collective-permute-start(f32[4,64,64]{2,1,0:T(8,128)S(1)} %add_select_fusion.1), channel_id=1, source_target_pairs={{0,256},{16,272},{32,288},{48,304},{64,320},{80,336},{96,352},{112... | collective-permute-start | bytes 196616 | tf_op jit(solution)/shard_map/ppermute | solution.py:18
  289.5 8.7 %copy-start.1 = (bf16[1,16,2,128,256]{4,3,0,1,2:T(8,128)(2,1)S(1)}, bf16[1,16,2,128,256]{4,3,0,1,2:T(8,128)(2,1)}, u32[]{:S(2)}) copy-start(bf16[1,16,2,128,256]{4,3,0,1,2:T(8,128)(2,1)} %get-tuple-element.137) | copy-start | bytes 6291460
  299.7 7.7 %copy-start.31 = (f32[256]{0:T(256)S(1)}, f32[256]{0:T(256)}, u32[]{:S(2)}) copy-start(f32[256]{0:T(256)} %param.33) | copy-start | bytes 3076
  299.7 7.7 %copy-start.32 = (pred[256]{0:T(512)(128)(4,1)S(1)}, pred[256]{0:T(512)(128)(4,1)}, u32[]{:S(2)}) copy-start(pred[256]{0:T(512)(128)(4,1)} %concatenate.22) | copy-start | bytes 772
  (26 other events, 71.3 us)
Sparse Core Ops, SparseCore 0:
  12.5 85.6 all-gather.7
  101.8 58.8 all-gather.5
  162.8 33.1 all-gather.9
  315.1 83.9 reduce-scatter.1
where the time goes:
time: 409 us; the launch traced here: 407 us
  waiting for transfers between devices  232 us (57%)
  starting transfers between devices  72.5 us (18%)
  local copies, waits for them, and re-layouts  54.7 us (13%)
  matrix products  21.7 us (5%)
  between operations  14.5 us (4%)
  other arithmetic  11.6 us (3%)
    all_gather x2, waiting for transfers between devices, on_device(): blocks = lax.all_gather(lax.all_gather(blocks, 'z'), 'core')  80.3 us
    reduce_scatter x1, waiting for transfers between devices, on_device(): lax.psum_scatter(lax.dot_general(hidden, full_out, (((1,), (1,)), ((), ()...  80.1 us
    ppermute x12, starting transfers between devices, seq_shift(): return lax.ppermute(x, SEQ, pairs)  72.3 us
    all_gather x1, waiting for transfers between devices, on_device(): stacked = lax.all_gather(stacked, 'mp', axis=1, tiled=True)  60.9 us
    ppermute x12, waiting for transfers between devices, seq_shift(): return lax.ppermute(x, SEQ, pairs)  10.7 us
    unnamed x71, local copies, waits for them, and re-layouts  10.1 us
    dynamic_update_slice x4, local copies, waits for them, and re-layouts, continued_recurrence(): lax.scan(step, jnp.zeros((per_group_view, embedding_dimension, embedding_...  8.76 us
  transfers between devices with their start and end apart: 16, of which 10 were waited for; matrix products, arithmetic and copies ran while one was open for 14% of the time, Pallas kernels for 0%

commit v1 on v0

--- a/solution.py
+++ b/solution.py
@@ -144,7 +144,8 @@
     first = seq_index() == 0
     edge_row = jnp.where(first, preceding_entry_line[None, :], arrived)
     stacked = jnp.concatenate([continued_prompt_entries, padded_prompt_entries, edge_row], axis=0)
-    stacked = lax.all_gather(stacked, "mp", axis=1, tiled=True)
+    copies = jnp.concatenate([stacked] * lax.axis_size("mp"), axis=1)
+    stacked = lax.all_to_all(copies, "mp", 1, 1, tiled=True)
     current = stacked[: long_rows + padded_prompt_entries.shape[0]]
     edge_full = stacked[-1:]
     previous = shifted_rows(current, edge_full, long_rows, requests, slot_rows)

time: 409 us -> 420 us (1.027)
  waiting for transfers between devices: 232 us -> 204 us
  local copies, waits for them, and re-layouts: 54.7 us -> 80.9 us
  other arithmetic: 11.6 us -> 30.6 us
  starting transfers between devices: 72.5 us -> 67.8 us
    all_gather x1 -> x0, waiting for transfers between devices: 60.9 us -> none  [on_device(): stacked = lax.all_gather(stacked, 'mp', axis=1, tiled=True)]
    all_to_all x0 -> x1, waiting for transfers between devices: none -> 28.5 us  [on_device(): stacked = lax.all_to_all(copies, 'mp', 1, 1, tiled=True)]
    convert_element_type x0 -> x2, other arithmetic: none -> 12.7 us  [mix_rows(): (here + weight[None, :] * (previous.astype(jnp.float32) - here)).astype(j...]
    ppermute x12, starting transfers between devices: 72.3 us -> 60.5 us  [seq_shift(): return lax.ppermute(x, SEQ, pairs)]
    unnamed x71 -> x82, local copies, waits for them, and re-layouts: 10.1 us -> 18.4 us
    all_to_all x0 -> x1, starting transfers between devices: none -> 7.24 us  [on_device(): stacked = lax.all_to_all(copies, 'mp', 1, 1, tiled=True)]
    all_gather x2, waiting for transfers between devices: 80.3 us -> 85.8 us  [on_device(): blocks = lax.all_gather(lax.all_gather(blocks, 'z'), 'core')]
    ppermute x12, waiting for transfers between devices: 10.7 us -> 5.83 us  [seq_shift(): return lax.ppermute(x, SEQ, pairs)]
  transfers between devices with their start and end apart: 16 -> 16, of which waited for: 10 -> 7; matrix products, arithmetic and copies ran while one was open for 14% -> 26% of each run, Pallas kernels for 0% -> 0%
where the time goes in v1:
time: 420 us; the launch traced here: 418 us
  waiting for transfers between devices  204 us (49%)
  local copies, waits for them, and re-layouts  80.9 us (19%)
  starting transfers between devices  67.8 us (16%)
  other arithmetic  30.6 us (7%)
  matrix products  19.2 us (5%)
  between operations  14.5 us (3%)
    all_gather x2, waiting for transfers between devices, on_device(): blocks = lax.all_gather(lax.all_gather(blocks, 'z'), 'core')  85.8 us
    reduce_scatter x1, waiting for transfers between devices, on_device(): lax.psum_scatter(lax.dot_general(hidden, full_out, (((1,), (1,)), ((), ()...  84.3 us
    ppermute x12, starting transfers between devices, seq_shift(): return lax.ppermute(x, SEQ, pairs)  60.5 us
    all_to_all x1, waiting for transfers between devices, on_device(): stacked = lax.all_to_all(copies, 'mp', 1, 1, tiled=True)  28.5 us
    unnamed x82, local copies, waits for them, and re-layouts  18.4 us
    convert_element_type x2, other arithmetic, mix_rows(): (here + weight[None, :] * (previous.astype(jnp.float32) - here)).astype(j...  12.7 us
    slice x5, local copies, waits for them, and re-layouts, on_device(): pieces = tuple((blocks[index] for index in range(4)))  9.57 us
    dynamic_update_slice x4, local copies, waits for them, and re-layouts, continued_recurrence(): lax.scan(step, jnp.zeros((per_group_view, embedding_dimension, embedding_...  8.78 us
  transfers between devices with their start and end apart: 16, of which 7 were waited for; matrix products, arithmetic and copies ran while one was open for 26% of the time, Pallas kernels for 0%

profile of v1, /device:TPU:2, one launch (start us, length us, event | category | flops | bytes accessed | tf_op | source)
XLA Modules:
  0.0 417.7 jit_solution(12254407610293321944)
XLA Ops:
  12.4 85.8 %all-gather.5.cloned.1.call-done = bf16[80,128,256]{2,1,0:T(8,128)(2,1)} async-done(((bf16[5,128,256]{2,1,0:T(8,128)(2,1)}), bf16[80,128,256]{2,1,0:T(8,128)(2,1)}) %all-gather.5.cloned.1.call-update) | async-done | bytes 5242896 | tf_op jit(solution)/shard_map/all_gather | solution.py:165
  104.4 7.2 %all-to-all-start = ((bf16[257,16,256]{2,0,1:T(8,128)(2,1)}), bf16[257,16,256]{2,0,1:T(8,128)(2,1)S(1)}, u32[]{:S(2)}, u32[]{:S(2)}) async-start(bf16[257,16,256]{2,0,1:T(8,128)(2,1)} %copy.211), calls=%async_computation | async-start | bytes 4325376 | tf_op jit(solution)/shard_map/all_to_all | solution.py:148
  113.8 28.5 %all-to-all-done = bf16[257,16,256]{2,0,1:T(8,128)(2,1)S(1)} async-done(((bf16[257,16,256]{2,0,1:T(8,128)(2,1)}), bf16[257,16,256]{2,0,1:T(8,128)(2,1)S(1)}, u32[]{:S(2)}, u32[]{:S(2)}) %all-to-all-start) | async-done | bytes 2105376 | tf_op jit(solution)/shard_map/all_to_all | solution.py:148
  154.3 2.8 copy.257
  161.8 4.5 %fusion.22 = bf16[256,4096]{0,1:T(8,128)(2,1)} fusion(bf16[256,16,256]{0,2,1:T(8,128)(2,1)S(1)} %copy.257, bf16[128,4096]{0,1:T(8,128)(2,1)} %copy.216, bf16[127,4096]{0,1:T(8,128)(2,1)} %bitcast.167, bf16[1,4096]{0,1:T(8,128)(2,1)} %bitcast.166, f32[4096]{0:T(1024)S(1)} %bitcast.187), kind=kLoop, calls=%fused_computation.44 | loop fusion | flops 11534336 | bytes 6307840 | tf_op jit(solution)/shard_map/convert_element_type | solution.py:36
  169.8 2.6 collective-permute-start.1
  178.4 2.6 copy.217
  183.7 8.1 %fusion.20 = (bf16[256,16,256]{0,2,1:T(8,128)(2,1)}, bf16[256,16,256]{0,2,1:T(8,128)(2,1)}, bf16[256,16,256]{0,2,1:T(8,128)(2,1)}, bf16[256,16,256]{0,2,1:T(8,128)(2,1)}) fusion(bf16[256,16,256]{0,2,1:T(8,128)(2,1)S(1)} %copy.257, f32[16,256]{1,0:T(8,128)S(1)} %mul.267, bf16[128,16,256]{0,2,1:T(8,128)(2,1)} %copy.217, bf16[127,16,256]{0,2,1:T(8,128)(2,1)} %copy.259, ...), kind=kLoop, calls=%fused_computation.40 | loop fusion | flops 20971520 | bytes 12648448 | tf_op jit(solution)/shard_map/convert_element_type | solution.py:36
  192.8 3.0 collective-permute-start.3
  197.6 4.5 %collective-permute-start.4 = (f32[4,64]{1,0:T(4,128)S(1)}, f32[4,64]{1,0:T(4,128)S(1)}, u32[]{:S(2)}, u32[]{:S(2)}) collective-permute-start(f32[4,64]{1,0:T(4,128)S(1)} %get-tuple-element.146), channel_id=1, source_target_pairs={{0,64},{16,80},{32,96},{48,112},{64,128},{80,144},{96,160},{112,17... | collective-permute-start | bytes 3080 | tf_op jit(solution)/shard_map/ppermute | solution.py:18
  205.7 7.3 %collective-permute-start.5 = (f32[4,64]{1,0:T(4,128)S(1)}, f32[4,64]{1,0:T(4,128)S(1)}, u32[]{:S(2)}, u32[]{:S(2)}) collective-permute-start(f32[4,64]{1,0:T(4,128)S(1)} %get-tuple-element.144), channel_id=1, source_target_pairs={{0,128},{16,144},{32,160},{48,176},{64,192},{80,208},{96,224},{112... | collective-permute-start | bytes 3080 | tf_op jit(solution)/shard_map/ppermute | solution.py:18
  212.9 5.8 %fusion.62 = (bf16[1,16,2,128,256]{4,3,0,1,2:T(8,128)(2,1)}, bf16[1,16,2,128,256]{4,3,0,1,2:T(8,128)(2,1)S(1)}, bf16[1,16,2,128,256]{4,3,0,1,2:T(8,128)(2,1)S(1)...) fusion(bf16[5,16,2,128,256]{4,3,0,1,2:T(8,128)(2,1)} %bitcast.163), kind=kLoop, calls=%fused_computation.146 | loop fusion | bytes 20971520 | tf_op jit(solution)/shard_map/slice | solution.py:168
  228.3 18.7 %while.13 = (s32[]{:T(128)}, f32[4,64,64]{2,1,0:T(8,128)S(1)}, f32[2,64,4,64]{1,0,3,2:T(2,128)}, f32[2,64,4,64]{1,0,3,2:T(2,128)S(1)}, f32[2,64,4,64]{3,2,1,0:T(...) while((s32[]{:T(128)}, f32[4,64,64]{2,1,0:T(8,128)S(1)}, ...), condition=%wide.region_3.4_spmd.clone, body=%wide.region_0.3_spmd.clone.sunk | while | flops 51646208 | bytes 2444424 | solution.py:96
  233.3 4.3 %dynamic_update_slice.6 = f32[2,64,4,64]{1,0,3,2:T(2,128)} dynamic-update-slice(f32[2,64,4,64]{1,0,3,2:T(2,128)} %get-tuple-element.255, f32[1,64,4,64]{1,0,3,2:T(1,128)S(1)} %copy.313, s32[]{:T(128)S(6)} %copy.337, s32[]{:T(128)} %constant.28.clone.1..sunk, s32[]{:T(128)} %constant.28.clone.1..sunk, s32[]{:T(128)} %constant.28.clone.1..sunk) | dynamic-update-slice | bytes 131076 | tf_op jit(solution)/shard_map/while/body/jit(dynamic_update_index_in_dim)/dynamic_update_slice | solution.py:96
  242.7 4.3 %dynamic_update_slice.6 = f32[2,64,4,64]{1,0,3,2:T(2,128)} dynamic-update-slice(f32[2,64,4,64]{1,0,3,2:T(2,128)} %get-tuple-element.255, f32[1,64,4,64]{1,0,3,2:T(1,128)S(1)} %copy.313, s32[]{:T(128)S(6)} %copy.337, s32[]{:T(128)} %constant.28.clone.1..sunk, s32[]{:T(128)} %constant.28.clone.1..sunk, s32[]{:T(128)} %constant.28.clone.1..sunk) | dynamic-update-slice | bytes 131076 | tf_op jit(solution)/shard_map/while/body/jit(dynamic_update_index_in_dim)/dynamic_update_slice | solution.py:96
  253.9 2.7 exponential_multiply_fusion
  256.8 6.2 %collective-permute-start.8 = (f32[4,64,64]{2,1,0:T(8,128)S(1)}, f32[4,64,64]{2,1,0:T(8,128)}, u32[]{:S(2)}, u32[]{:S(2)}) collective-permute-start(f32[4,64,64]{2,1,0:T(8,128)S(1)} %add_select_fusion.4), channel_id=1, source_target_pairs={{0,32},{16,48},{32,64},{48,80},{64,96},{80,112},{96,128},{112,144}... | collective-permute-start | bytes 196616 | tf_op jit(solution)/shard_map/ppermute | solution.py:18
  267.4 3.3 collective-permute-start.9
  271.3 3.1 collective-permute-done.9
  274.5 12.8 %collective-permute-start.10 = (f32[4,64,64]{2,1,0:T(8,128)S(1)}, f32[4,64,64]{2,1,0:T(8,128)}, u32[]{:S(2)}, u32[]{:S(2)}) collective-permute-start(f32[4,64,64]{2,1,0:T(8,128)S(1)} %add_select_fusion.2), channel_id=1, source_target_pairs={{0,128},{16,144},{32,160},{48,176},{64,192},{80,208},{96,224},{112... | collective-permute-start | bytes 196616 | tf_op jit(solution)/shard_map/ppermute | solution.py:18
  290.2 14.0 %collective-permute-start.11 = (f32[4,64,64]{2,1,0:T(8,128)S(1)}, f32[4,64,64]{2,1,0:T(8,128)}, u32[]{:S(2)}, u32[]{:S(2)}) collective-permute-start(f32[4,64,64]{2,1,0:T(8,128)S(1)} %add_select_fusion.1), channel_id=1, source_target_pairs={{0,256},{16,272},{32,288},{48,304},{64,320},{80,336},{96,352},{112... | collective-permute-start | bytes 196616 | tf_op jit(solution)/shard_map/ppermute | solution.py:18
  306.1 3.1 copy.245
  314.3 6.6 %fusion.43 = f32[256,4096]{1,0:T(8,128)} fusion(bf16[4096,256]{1,0:T(8,128)(2,1)} %bitcast.170, f32[256,256]{1,0:T(8,128)S(1)} %copy.244, f32[256,256]{1,0:T(8,128)S(1)} %copy.243, f32[128,256]{1,0:T(8,128)S(1)} %concatenate.41, f32[128,256]{1,0:T(8,128)S(1)} %copy.241, f32[256]{0:T(256)S(1)} %copy-done.32, f32[256]{0:T(256)S(1)} %copy-done.33, ...), kind=kOutput, calls=%fused_computation.87 | convolution fusion | flops 1074528256 | bytes 11274496 | tf_op jit(solution)/shard_map/dot_general | solution.py:244
  325.3 84.3 %reduce-scatter.2.cloned.1.call-done = f32[16,4096]{1,0:T(8,128)} async-done(((f32[256,4096]{1,0:T(8,128)}), f32[16,4096]{1,0:T(8,128)}) %reduce-scatter.2.cloned.1.call-update) | async-done | bytes 262160 | tf_op jit(solution)/shard_map/reduce_scatter | solution.py:243
  (236 shorter events, 95.4 us)
Async XLA Ops:
  7.2 159.2 %copy-start = (bf16[4096,128]{1,0:T(8,128)(2,1)S(1)}, bf16[4096,128]{1,0:T(8,128)(2,1)}, u32[]{:S(2)}) copy-start(bf16[4096,128]{1,0:T(8,128)(2,1)} %param.30) | copy-start | bytes 3145732
  7.2 91.1 %all-gather.5.cloned.1.call-start = ((), (), s32[]{:S(2)}) async-start(), calls=%async_computation.3 | async-start | bytes 5570560 | tf_op jit(solution)/shard_map/all_gather | solution.py:165
  12.4 200.6 %all-gather.7.cloned.1.call-start = ((), (), s32[]{:S(2)}) async-start(), calls=%async_computation.4 | async-start | bytes 15728640 | tf_op jit(solution)/shard_map/all_gather | solution.py:165
  99.1 2.1 collective-permute-start
  104.4 37.8 %all-to-all-start = ((bf16[257,16,256]{2,0,1:T(8,128)(2,1)}), bf16[257,16,256]{2,0,1:T(8,128)(2,1)S(1)}, u32[]{:S(2)}, u32[]{:S(2)}) async-start(bf16[257,16,256]{2,0,1:T(8,128)(2,1)} %copy.211), calls=%async_computation | async-start | bytes 4325376 | tf_op jit(solution)/shard_map/all_to_all | solution.py:148
  111.7 297.9 %reduce-scatter.2.cloned.1.call-start = ((), (), s32[]{:S(2)}) async-start(), calls=%async_computation.2 | async-start | bytes 4456448 | tf_op jit(solution)/shard_map/reduce_scatter | solution.py:243
  169.8 11.3 %collective-permute-start.1 = (f32[4,64]{1,0:T(4,128)S(1)}, f32[4,64]{1,0:T(4,128)S(1)}, u32[]{:S(2)}, u32[]{:S(2)}) collective-permute-start(f32[4,64]{1,0:T(4,128)S(1)} %reduce_sum.48), channel_id=1, source_target_pairs={{0,16},{16,32},{32,48},{48,64},{64,80},{80,96},{96,112},{112,128},... | collective-permute-start | bytes 3080 | tf_op jit(solution)/shard_map/ppermute | solution.py:18
  181.6 10.6 %collective-permute-start.2 = (f32[4,64]{1,0:T(4,128)S(1)}, f32[4,64]{1,0:T(4,128)S(1)}, u32[]{:S(2)}, u32[]{:S(2)}) collective-permute-start(f32[4,64]{1,0:T(4,128)S(1)} %get-tuple-element.150), channel_id=1, source_target_pairs={{0,16},{16,32},{32,48},{48,64},{64,80},{80,96},{96,112},{112,128},... | collective-permute-start | bytes 3080 | tf_op jit(solution)/shard_map/ppermute | solution.py:18
  192.2 26.6 %copy-start.8 = (f32[2,64,4,64]{3,2,1,0:T(4,128)}, f32[2,64,4,64]{3,2,1,0:T(4,128)S(1)}, u32[]{:S(2)}) copy-start(f32[2,64,4,64]{3,2,1,0:T(4,128)S(1)} %copy.231) | copy-start | bytes 393220
  192.8 4.3 %collective-permute-start.3 = (f32[4,64]{1,0:T(4,128)S(1)}, f32[4,64]{1,0:T(4,128)S(1)}, u32[]{:S(2)}, u32[]{:S(2)}) collective-permute-start(f32[4,64]{1,0:T(4,128)S(1)} %get-tuple-element.148), channel_id=1, source_target_pairs={{0,32},{16,48},{32,64},{48,80},{64,96},{80,112},{96,128},{112,144}... | collective-permute-start | bytes 3080 | tf_op jit(solution)/shard_map/ppermute | solution.py:18
  196.0 22.8 %copy-start.16 = (f32[2,64,4,64]{3,2,1,0:T(4,128)}, f32[2,64,4,64]{3,2,1,0:T(4,128)S(1)}, u32[]{:S(2)}) copy-start(f32[2,64,4,64]{3,2,1,0:T(4,128)S(1)} %fusion.40) | copy-start | bytes 393220
  197.6 7.4 %collective-permute-start.4 = (f32[4,64]{1,0:T(4,128)S(1)}, f32[4,64]{1,0:T(4,128)S(1)}, u32[]{:S(2)}, u32[]{:S(2)}) collective-permute-start(f32[4,64]{1,0:T(4,128)S(1)} %get-tuple-element.146), channel_id=1, source_target_pairs={{0,64},{16,80},{32,96},{48,112},{64,128},{80,144},{96,160},{112,17... | collective-permute-start | bytes 3080 | tf_op jit(solution)/shard_map/ppermute | solution.py:18
  205.7 42.8 %collective-permute-start.5 = (f32[4,64]{1,0:T(4,128)S(1)}, f32[4,64]{1,0:T(4,128)S(1)}, u32[]{:S(2)}, u32[]{:S(2)}) collective-permute-start(f32[4,64]{1,0:T(4,128)S(1)} %get-tuple-element.144), channel_id=1, source_target_pairs={{0,128},{16,144},{32,160},{48,176},{64,192},{80,208},{96,224},{112... | collective-permute-start | bytes 3080 | tf_op jit(solution)/shard_map/ppermute | solution.py:18
  247.0 3.8 collective-permute-start.6
  251.7 4.9 %collective-permute-start.7 = (f32[4,64,64]{2,1,0:T(8,128)S(1)}, f32[4,64,64]{2,1,0:T(8,128)S(1)}, u32[]{:S(2)}, u32[]{:S(2)}) collective-permute-start(f32[4,64,64]{2,1,0:T(8,128)S(1)} %broadcast_select_fusion), channel_id=1, source_target_pairs={{0,16},{16,32},{32,48},{48,64},{64,80},{80,96},{96,112},{112,128},... | collective-permute-start | bytes 196616 | tf_op jit(solution)/shard_map/ppermute | solution.py:18
  256.7 31.4 %copy-start.13 = (f32[128,256]{0,1:T(8,128)S(1)}, f32[128,256]{0,1:T(8,128)}, u32[]{:S(2)}) copy-start(f32[128,256]{0,1:T(8,128)} %copy-done.12) | copy-start | bytes 393220
  256.8 9.6 %collective-permute-start.8 = (f32[4,64,64]{2,1,0:T(8,128)S(1)}, f32[4,64,64]{2,1,0:T(8,128)}, u32[]{:S(2)}, u32[]{:S(2)}) collective-permute-start(f32[4,64,64]{2,1,0:T(8,128)S(1)} %add_select_fusion.4), channel_id=1, source_target_pairs={{0,32},{16,48},{32,64},{48,80},{64,96},{80,112},{96,128},{112,144}... | collective-permute-start | bytes 196616 | tf_op jit(solution)/shard_map/ppermute | solution.py:18
  262.9 26.2 %copy-start.27 = (f32[4,64]{1,0:T(4,128)S(1)}, f32[4,64]{1,0:T(4,128)}, u32[]{:S(2)}) copy-start(f32[4,64]{1,0:T(4,128)} %get-tuple-element.143) | copy-start | bytes 3076
  263.5 40.7 %copy-start.7 = (f32[128,4,64]{2,1,0:T(4,128)S(1)}, f32[128,4,64]{2,1,0:T(4,128)}, u32[]{:S(2)}) copy-start(f32[128,4,64]{2,1,0:T(4,128)} %copy.226) | copy-start | bytes 393220
  267.4 7.0 %collective-permute-start.9 = (f32[4,64,64]{2,1,0:T(8,128)S(1)}, f32[4,64,64]{2,1,0:T(8,128)S(1)}, u32[]{:S(2)}, u32[]{:S(2)}) collective-permute-start(f32[4,64,64]{2,1,0:T(8,128)S(1)} %add_select_fusion.3), channel_id=1, source_target_pairs={{0,64},{16,80},{32,96},{48,112},{64,128},{80,144},{96,160},{112,17... | collective-permute-start | bytes 196616 | tf_op jit(solution)/shard_map/ppermute | solution.py:18
  274.5 14.7 %collective-permute-start.10 = (f32[4,64,64]{2,1,0:T(8,128)S(1)}, f32[4,64,64]{2,1,0:T(8,128)}, u32[]{:S(2)}, u32[]{:S(2)}) collective-permute-start(f32[4,64,64]{2,1,0:T(8,128)S(1)} %add_select_fusion.2), channel_id=1, source_target_pairs={{0,128},{16,144},{32,160},{48,176},{64,192},{80,208},{96,224},{112... | collective-permute-start | bytes 196616 | tf_op jit(solution)/shard_map/ppermute | solution.py:18
  290.2 21.8 %copy-start.14 = (f32[4,64,64]{2,1,0:T(8,128)}, f32[4,64,64]{2,1,0:T(8,128)S(1)}, u32[]{:S(2)}) copy-start(f32[4,64,64]{2,1,0:T(8,128)S(1)} %add_select_fusion.1) | copy-start | bytes 196612
  290.2 21.8 %collective-permute-start.11 = (f32[4,64,64]{2,1,0:T(8,128)S(1)}, f32[4,64,64]{2,1,0:T(8,128)}, u32[]{:S(2)}, u32[]{:S(2)}) collective-permute-start(f32[4,64,64]{2,1,0:T(8,128)S(1)} %add_select_fusion.1), channel_id=1, source_target_pairs={{0,256},{16,272},{32,288},{48,304},{64,320},{80,336},{96,352},{112... | collective-permute-start | bytes 196616 | tf_op jit(solution)/shard_map/ppermute | solution.py:18
  320.9 90.3 %copy-start.1 = (bf16[4096,128]{1,0:T(8,128)(2,1)S(1)}, bf16[4096,128]{1,0:T(8,128)(2,1)}, u32[]{:S(2)}) copy-start(bf16[4096,128]{1,0:T(8,128)(2,1)} %param.30) | copy-start | bytes 3145732
  (28 other events, 168.3 us)
Sparse Core Ops, SparseCore 0:
  12.5 85.6 all-gather.4
  100.3 29.2 all-gather.6
  321.1 88.4 reduce-scatter.1
